TPU v7x, 32 devices: a whole 2x2x4 slice. The times are simulated.
32 devices in a mesh: frame: 8 (over y, x, core), head: 4 (over z).
Axes of the slice: x: 2, y: 2, z: 4, core: 2. Of those that a mesh axis runs over, the one named last changes fastest.
Arguments:
- visual: bfloat16 [1024, 8192], P('frame'), may hold values from -6 to 6
- w_key: bfloat16 [8192, 1024], P(None, 'head'), may hold values from -0.0625 to 0.0625
- w_value: bfloat16 [8192, 1024], P(None, 'head'), may hold values from -0.0625 to 0.0625
- queries: float32 [256, 8192], P('frame', 'head'), may hold values from -100 to 100
- out_grad: float32 [256, 8192], P('frame', 'head'), may hold values from -6 to 6
Outputs:
- query_grad: float32 [256, 8192], P('frame', 'head')
- key_weight_grad: float32 [8192, 1024], P('frame', 'head')
- value_weight_grad: float32 [8192, 1024], P('frame', 'head')
- visual_grad: float32 [1024, 8192], P('frame', 'head')
All inputs are finite; a program needn't handle non-finite values.
Results may differ from a plain program's by a relative error of at most 0.009.
Values sent between devices are 32-bit elements; how exact they have to be, the bound alone decides.
A program may use at most 128 MiB of HBM per device.

v0:
```python
import jax
import jax.numpy as jnp
from jax import lax
from jax.sharding import PartitionSpec as P

HEAD_DIM = 128


def combined_all(part, axis, combine):
    gathered = jax.tree.map(lambda a: lax.all_gather(a, axis), part)

    def take(source):
        return jax.tree.map(lambda a: lax.dynamic_index_in_dim(a, source, 0, False), gathered)

    return lax.fori_loop(
        1, lax.axis_size(axis), lambda source, state: combine(state, take(source)), take(0)
    )


def partial_stats(query_blk, grad_blk, key_blk, value_blk):
    factor = HEAD_DIM ** (-0.5)
    scores = (
        jnp.einsum("sagd,nad->agsn", query_blk, key_blk, precision=lax.Precision.HIGHEST) * factor
    )
    dprob = jnp.einsum("sagd,nad->agsn", grad_blk, value_blk, precision=lax.Precision.HIGHEST)
    top_score = jnp.max(scores, axis=-1, keepdims=True)
    weights = jnp.exp(scores - top_score)
    total = jnp.sum(weights, axis=-1, keepdims=True)
    weighted = jnp.sum(weights * dprob, axis=-1, keepdims=True)
    return (scores, dprob, top_score, total, weighted)


def combine_stats(first, second):
    top_score = jnp.maximum(first[0], second[0])
    scale_one = jnp.exp(first[0] - top_score)
    scale_two = jnp.exp(second[0] - top_score)
    return (
        top_score,
        first[1] * scale_one + second[1] * scale_two,
        first[2] * scale_one + second[2] * scale_two,
    )


def finish(scores, dprob, log_total, delta, query_blk, grad_blk, key_blk):
    factor = HEAD_DIM ** (-0.5)
    probs = jnp.exp(scores - log_total)
    dscore = probs * (dprob - delta)
    query_part = (
        jnp.einsum("agsn,nad->sagd", dscore, key_blk, precision=lax.Precision.HIGHEST) * factor
    )
    key_part = (
        jnp.einsum("agsn,sagd->nad", dscore, query_blk, precision=lax.Precision.HIGHEST) * factor
    )
    value_part = jnp.einsum("agsn,sagd->nad", probs, grad_blk, precision=lax.Precision.HIGHEST)
    return (query_part, key_part, value_part)


def body(visual, w_key, w_value, queries, out_grad):
    keys = jnp.dot(visual, w_key, preferred_element_type=jnp.float32)
    values = jnp.dot(visual, w_value, preferred_element_type=jnp.float32)
    kv_local = w_key.shape[1] // HEAD_DIM
    per_group = queries.shape[1] // HEAD_DIM // kv_local
    vis_rows = visual.shape[0]
    all_query, all_grad = (
        lax.all_gather(queries, "frame", axis=0, tiled=True),
        lax.all_gather(out_grad, "frame", axis=0, tiled=True),
    )
    text_rows = all_query.shape[0]
    query_blk = all_query.reshape(text_rows, kv_local, per_group, HEAD_DIM)
    grad_blk = all_grad.reshape(text_rows, kv_local, per_group, HEAD_DIM)
    key_blk = keys.reshape(vis_rows, kv_local, HEAD_DIM)
    value_blk = values.reshape(vis_rows, kv_local, HEAD_DIM)
    scores, dprob, top_score, total, weighted = partial_stats(
        query_blk, grad_blk, key_blk, value_blk
    )
    top_all, total_all, weighted_all = combined_all(
        (top_score, total, weighted), "frame", combine_stats
    )
    log_total = top_all + jnp.log(total_all)
    delta = weighted_all / total_all
    query_part, key_part, value_part = finish(
        scores, dprob, log_total, delta, query_blk, grad_blk, key_blk
    )
    query_grad = lax.psum_scatter(
        query_part.reshape(text_rows, -1), "frame", scatter_dimension=0, tiled=True
    )
    key_grad = key_part.reshape(vis_rows, -1)
    value_grad = value_part.reshape(vis_rows, -1)
    key_low = key_grad.astype(jnp.bfloat16)
    value_low = value_grad.astype(jnp.bfloat16)
    key_weight_part = jnp.einsum("nd,nc->dc", visual, key_low, preferred_element_type=jnp.float32)
    value_weight_part = jnp.einsum(
        "nd,nc->dc", visual, value_low, preferred_element_type=jnp.float32
    )
    key_weight_grad, value_weight_grad = (
        lax.psum_scatter(key_weight_part, "frame", scatter_dimension=0, tiled=True),
        lax.psum_scatter(value_weight_part, "frame", scatter_dimension=0, tiled=True),
    )
    visual_part = jnp.einsum(
        "nc,dc->nd", key_low, w_key, preferred_element_type=jnp.float32
    ) + jnp.einsum("nc,dc->nd", value_low, w_value, preferred_element_type=jnp.float32)
    visual_grad = lax.psum_scatter(visual_part, "head", scatter_dimension=1, tiled=True)
    return (query_grad, key_weight_grad, value_weight_grad, visual_grad)


def solution(mesh):
    return jax.shard_map(
        body,
        mesh=mesh,
        in_specs=(
            P("frame", None),
            P(None, "head"),
            P(None, "head"),
            P("frame", "head"),
            P("frame", "head"),
        ),
        out_specs=(P("frame", "head"), P("frame", "head"), P("frame", "head"), P("frame", "head")),
        check_vma=False,
    )
```

profile of v0, /device:TPU:22, one launch (start us, length us, event | category | flops | bytes accessed | tf_op | source)
XLA Modules:
  0.0 383.6 jit_solution(5083664487156576952)
XLA Ops:
  7.2 0.7 all-gather.6.cloned.1.call-update
  8.0 0.7 all-gather.8.cloned.1.call-update
  8.7 0.0 reduce-scatter.9.cloned.1.call-start
  8.7 0.1 copy-done
  8.8 2.9 fusion.27
  11.7 0.1 reshape.30
  11.7 3.9 %fusion.26 = f32[128,256]{0,1:T(8,128)S(1)} fusion(bf16[128,8192]{1,0:T(8,128)(2,1)S(1)} %copy-done, bf16[8192,256]{1,0:T(8,128)(2,1)} %param.8), kind=kOutput, calls=%fused_computation.43 | convolution fusion | flops 536870912 | bytes 6422528 | tf_op jit(solution)/shard_map/dot_general | solution.py:59
  15.7 22.1 %all-gather.6.cloned.1.call-done = f32[256,2048]{1,0:T(8,128)} async-done(((f32[32,2048]{1,0:T(8,128)}), f32[256,2048]{1,0:T(8,128)}) %all-gather.6.cloned.1.call-update) | async-done | bytes 2097168 | tf_op jit(solution)/shard_map/all_gather | solution.py:65
  37.8 3.0 copy.33
  40.7 4.9 %bitcast_reduce_fusion = (f32[2,8,256]{2,1,0:T(8,128)S(1)}, f32[2,128,256,8]{2,1,3,0:T(8,128)}) fusion(f32[128,2,128,1]{0,2,3,1:T(8,128)S(1)} %bitcast.132, f32[256,2,8,128]{0,3,2,1:T(8,128)} %bitcast.126), kind=kOutput, calls=%fused_computation.22 | convolution fusion | flops 806350848 | bytes 4341760 | tf_op jit(solution)/shard_map/sagd,nad->agsn/dot_general | solution.py:23
  45.7 9.3 %all-gather = f32[16,8,256]{2,1,0:T(8,128)S(1)} all-gather(f32[2,8,256]{2,1,0:T(8,128)S(1)} %get-tuple-element.226), channel_id=2, replica_groups=mesh['frame'=8,'head'=4] {'frame'}, dimensions={0}, use_global_device_ids=true | all-gather | bytes 147456 | tf_op jit(solution)/shard_map/all_gather | solution.py:10
  55.0 12.8 %all-gather.8.cloned.1.call-done = f32[256,2048]{1,0:T(8,128)} async-done(((f32[32,2048]{1,0:T(8,128)}), f32[256,2048]{1,0:T(8,128)}) %all-gather.8.cloned.1.call-update) | async-done | bytes 2097168 | tf_op jit(solution)/shard_map/all_gather | solution.py:66
  67.8 2.9 copy.36
  70.7 5.7 %fusion.5 = (f32[2,8,256]{2,1,0:T(8,128)S(1)}, f32[2,8,256]{2,1,0:T(8,128)S(1)}, f32[2,128,256,8]{2,1,3,0:T(8,128)}) fusion(f32[2,128,256,8]{2,1,3,0:T(8,128)} %get-tuple-element.227, f32[2,8,256]{2,1,0:T(8,128)S(1)} %get-tuple-element.226, f32[256,2,8,128]{0,3,2,1:T(8,128)} %bitcast.128, f32[128,2,128,1]{2,1,0,3:T(2,128)S(1)} %bitcast.140), kind=kOutput, calls=%fused_computation.18 | convolution fusion | flops 807395328 | bytes 6471680 | tf_op jit(solution)/shard_map/sagd,nad->agsn/dot_general | solution.py:25
  76.5 9.2 %all-gather.2 = f32[16,8,256]{2,1,0:T(8,128)S(1)} all-gather(f32[2,8,256]{2,1,0:T(8,128)S(1)} %get-tuple-element.204), channel_id=4, replica_groups=mesh['frame'=8,'head'=4] {'frame'}, dimensions={0}, use_global_device_ids=true | all-gather | bytes 147456 | tf_op jit(solution)/shard_map/all_gather | solution.py:10
  85.6 8.4 %all-gather.1 = f32[16,8,256]{2,1,0:T(8,128)S(1)} all-gather(f32[2,8,256]{2,1,0:T(8,128)S(1)} %get-tuple-element.205), channel_id=3, replica_groups=mesh['frame'=8,'head'=4] {'frame'}, dimensions={0}, use_global_device_ids=true | all-gather | bytes 147456 | tf_op jit(solution)/shard_map/all_gather | solution.py:10
  94.1 1.5 while.19
  94.2 0.1 fusion.49
  94.2 0.1 fusion.50
  94.4 0.1 fusion.49
  94.5 0.1 fusion.50
  94.6 0.1 fusion.49
  94.7 0.1 fusion.50
  94.8 0.1 fusion.49
  94.9 0.1 fusion.50
  95.0 0.1 fusion.49
  95.1 0.1 fusion.50
  95.2 0.1 fusion.49
  95.3 0.1 fusion.50
  95.4 0.1 fusion.49
  95.5 0.1 fusion.50
  95.6 4.6 %fusion.17 = bf16[2,128,128]{1,2,0:T(8,128)(2,1)S(1)} fusion(f32[256,2,8,128]{0,3,2,1:T(8,128)} %bitcast.129, f32[2,128,256,8]{2,1,3,0:T(8,128)} %get-tuple-element.227, f32[2,8,256]{2,1,0:T(8,128)S(1)} %get-tuple-element.230), kind=kOutput, calls=%fused_computation.33 | convolution fusion | flops 805863424 | bytes 4276224 | tf_op jit(solution)/shard_map/agsn,sagd->nad/dot_general | solution.py:54
  100.2 4.5 %convolution_bitcast_fusion = f32[8192,256]{0,1:T(8,128)} fusion(bf16[128,256]{0,1:T(8,128)(2,1)S(1)} %bitcast.136, bf16[128,8192]{1,0:T(8,128)(2,1)S(1)} %copy-done), kind=kOutput, calls=%fused_computation.13 | convolution fusion | flops 536870912 | bytes 10551296 | tf_op jit(solution)/shard_map/nd,nc->dc/dot_general | solution.py:92
  104.7 0.0 reduce-scatter.7.cloned.1.call-start
  104.7 5.4 %fusion.16 = bf16[2,128,128]{1,2,0:T(8,128)(2,1)S(1)} fusion(f32[256,2,8,128]{0,3,2,1:T(8,128)} %bitcast.127, f32[2,128,256,8]{2,1,3,0:T(8,128)} %get-tuple-element.228, f32[2,128,256,8]{2,1,3,0:T(8,128)} %get-tuple-element.227, f32[2,8,256]{2,1,0:T(8,128)S(1)} %get-tuple-element.229, f32[2,8,256]{2,1,0:T(8,128)S(1)} %get-tuple-element.230), kind=kOutput, calls=%fused_computation.32 | convolution fusion | flops 806944768 | bytes 6389760 | tf_op jit(solution)/shard_map/agsn,sagd->nad/dot_general | solution.py:52
  110.1 5.1 %convolution_bitcast_fusion.1 = f32[8192,256]{0,1:T(8,128)} fusion(bf16[128,256]{0,1:T(8,128)(2,1)S(1)} %bitcast.138, bf16[128,8192]{1,0:T(8,128)(2,1)S(1)} %copy-done), kind=kOutput, calls=%fused_computation.14 | convolution fusion | flops 536870912 | bytes 10551296 | tf_op jit(solution)/shard_map/nd,nc->dc/dot_general | solution.py:91
  115.2 0.0 reduce-scatter.5.cloned.1.call-start
  115.3 6.5 %convolution_multiply_fusion = f32[2,128,8,256]{3,1,2,0:T(8,128)} fusion(f32[128,2,128,1]{0,2,3,1:T(8,128)S(1)} %bitcast.133, f32[2,128,256,8]{2,1,3,0:T(8,128)} %get-tuple-element.228, f32[2,128,256,8]{2,1,3,0:T(8,128)} %get-tuple-element.227, f32[2,8,256]{2,1,0:T(8,128)S(1)} %get-tuple-element.229, f32[2,8,256]{2,1,0:T(8,128)S(1)} %get-tuple-element.230), kind=kOutput, calls=%fused_computation.27 | convolution fusion | flops 807403520 | bytes 6455296 | tf_op jit(solution)/shard_map/agsn,nad->sagd/dot_general | solution.py:49
  121.8 3.0 copy.47
  124.8 0.3 reduce-scatter.11.cloned.1.call-start
  125.1 3.8 fusion.28
  128.9 3.6 convolution_add_fusion
  132.6 43.7 %reduce-scatter.9.cloned.1.call-done = f32[1024,256]{0,1:T(8,128)} async-done(((f32[8192,256]{0,1:T(8,128)}), f32[1024,256]{0,1:T(8,128)}) %reduce-scatter.9.cloned.1.call-update) | async-done | bytes 1048592 | tf_op jit(solution)/shard_map/reduce_scatter | solution.py:97
  176.2 2.5 copy.51
  178.8 72.2 %reduce-scatter.7.cloned.1.call-done = f32[1024,256]{0,1:T(8,128)} async-done(((f32[8192,256]{0,1:T(8,128)}), f32[1024,256]{0,1:T(8,128)}) %reduce-scatter.7.cloned.1.call-update) | async-done | bytes 1048592 | tf_op jit(solution)/shard_map/reduce_scatter | solution.py:96
  251.0 2.5 copy.50
  253.5 42.3 %reduce-scatter.5.cloned.1.call-done = f32[32,2048]{1,0:T(8,128)} async-done(((f32[256,2048]{1,0:T(8,128)}), f32[32,2048]{1,0:T(8,128)}) %reduce-scatter.5.cloned.1.call-update) | async-done | bytes 262160 | tf_op jit(solution)/shard_map/reduce_scatter | solution.py:84
  295.8 81.0 %reduce-scatter.11.cloned.1.call-done = f32[128,2048]{1,0:T(8,128)} async-done(((f32[128,8192]{1,0:T(8,128)}), f32[128,2048]{1,0:T(8,128)}) %reduce-scatter.11.cloned.1.call-update) | async-done | bytes 1048592 | tf_op jit(solution)/shard_map/reduce_scatter | solution.py:102
  (38 shorter events, 0.4 us)
Async XLA Ops:
  7.2 1.6 copy-start
  7.2 30.6 %all-gather.6.cloned.1.call-start = ((), (), s32[]{:S(2)}) async-start(), calls=%async_computation.4 | async-start | bytes 2359296 | tf_op jit(solution)/shard_map/all_gather | solution.py:65
  7.9 59.9 %all-gather.8.cloned.1.call-start = ((), (), s32[]{:S(2)}) async-start(), calls=%async_computation.5 | async-start | bytes 2359296 | tf_op jit(solution)/shard_map/all_gather | solution.py:66
  8.7 167.6 %reduce-scatter.9.cloned.1.call-start = ((), (), s32[]{:S(2)}) async-start(), calls=%async_computation.8 | async-start | bytes 9437184 | tf_op jit(solution)/shard_map/reduce_scatter | solution.py:97
  104.7 146.3 %reduce-scatter.7.cloned.1.call-start = ((), (), s32[]{:S(2)}) async-start(), calls=%async_computation.7 | async-start | bytes 9437184 | tf_op jit(solution)/shard_map/reduce_scatter | solution.py:96
  115.2 180.6 %reduce-scatter.5.cloned.1.call-start = ((), (), s32[]{:S(2)}) async-start(), calls=%async_computation.6 | async-start | bytes 2359296 | tf_op jit(solution)/shard_map/reduce_scatter | solution.py:84
  124.8 252.0 %reduce-scatter.11.cloned.1.call-start = ((), (), s32[]{:S(2)}) async-start(), calls=%async_computation.9 | async-start | bytes 5242880 | tf_op jit(solution)/shard_map/reduce_scatter | solution.py:102
  125.1 3.8 %copy-start.1 = (bf16[8192,256]{1,0:T(8,128)(2,1)S(1)}, bf16[8192,256]{1,0:T(8,128)(2,1)}, u32[]{:S(2)}) copy-start(bf16[8192,256]{1,0:T(8,128)(2,1)} %param.9) | copy-start | bytes 12582916
Sparse Core Ops, SparseCore 0:
  9.9 27.8 all-gather.5
  39.6 28.1 all-gather.7
  104.8 71.3 reduce-scatter.8
  179.5 71.3 reduce-scatter.6
  254.7 41.0 reduce-scatter.4
  298.5 78.2 reduce-scatter.10
where the time goes:
time: 385 us; the launch traced here: 384 us
  waiting for transfers between devices  276 us (72%)
  matrix products  50.9 us (13%)
  blocking collectives  26.9 us (7%)
  local copies, waits for them, and re-layouts  14.3 us (4%)
  between operations  14.2 us (4%)
    reduce_scatter x1, waiting for transfers between devices, body(): lax.psum_scatter(visual_part, 'head', scatter_dimension=1, tiled=True)  81 us
    reduce_scatter x1, waiting for transfers between devices, body(): lax.psum_scatter(key_weight_part, 'frame', scatter_dimension=0, tiled=True)  72.2 us
    reduce_scatter x1, waiting for transfers between devices, body(): lax.psum_scatter(value_weight_part, 'frame', scatter_dimension=0, tiled=T...  43.7 us
    reduce_scatter x1, waiting for transfers between devices, body(): lax.psum_scatter(query_part.reshape(text_rows, -1), 'frame', scatter_dime...  42.3 us
    all_gather x3, blocking collectives, combined_all(): gathered = jax.tree.map(lambda a: lax.all_gather(a, axis), part)  26.9 us
    all_gather x1, waiting for transfers between devices, body(): lax.all_gather(queries, 'frame', axis=0, tiled=True)  22.1 us
    all_gather x1, waiting for transfers between devices, body(): lax.all_gather(out_grad, 'frame', axis=0, tiled=True)  12.8 us
  transfers between devices with their start and end apart: 6, of which 6 were waited for; matrix products, arithmetic and copies ran while one was open for 12% of the time, Pallas kernels for 0%

commit v1 on v0

v1 whole, which is shorter than its diff:
```python
import functools

import jax
import jax.numpy as jnp
from jax import lax
from jax.experimental import pallas as pl
from jax.experimental.pallas import tpu as pltpu
from jax.sharding import PartitionSpec as P

HEAD_DIM = 128
MESH = pl.DeviceIdType.MESH
CHUNKS = 8
F32, BF16 = jnp.float32, jnp.bfloat16


def halves(a):
    high = a.astype(BF16)
    return high, (a - high.astype(F32)).astype(BF16)


def product(a, b, dims):
    (ah, al), (bh, bl) = a, b
    dot = functools.partial(
        lax.dot_general, dimension_numbers=(dims, ((), ())), preferred_element_type=F32
    )
    return dot(ah, bh) + (dot(ah, bl) + dot(al, bh))


def kernel(
    n, nh, vis, wk_any, wv_any, q, g, qg_out, kwg_out, vwg_out, vg_out,
    wk, wv, visf, visl, vist, ql, gl, kvs, kvl, parts, partl, kgs, agl, qgs, qgl, vgp, vgl,
    w_sem, q_sems, g_sems, kv_sems, v0_sems, v1_sems, part_sems, qg_sems, ag_sems, z_sems,
):
    me, my_head = lax.axis_index("frame"), lax.axis_index("head")
    rows, depth = vis.shape
    cols = wk.shape[1]
    kv_local = cols // HEAD_DIM
    text_part, width = ql.shape[1], ql.shape[2]
    split = q.shape[0] // text_part
    heads = width // HEAD_DIM
    share = n // kv_local
    dn, dh = depth // n, depth // nh
    chunk = depth // CHUNKS
    half = rows // 2
    factor = HEAD_DIM ** (-0.5)

    def frame_copy(src, dst, sems, slot_send, slot_recv, target):
        return pltpu.make_async_remote_copy(
            src_ref=src, dst_ref=dst, send_sem=sems.at[0, slot_send],
            recv_sem=sems.at[1, slot_recv], device_id={"frame": target}, device_id_type=MESH,
        )

    def peer(k):
        return lax.rem(me + k, n)

    def source(k):
        return lax.rem(me + n - k, n)

    loads = []
    for c in range(CHUNKS):
        at = pl.ds(c * chunk, chunk)
        for i, (src, dst) in enumerate(((wk_any, wk), (wv_any, wv))):
            loads.append(pltpu.make_async_copy(src.at[at], dst.at[at], w_sem.at[i, c]))
            loads[-1].start()

    barrier = pltpu.get_barrier_semaphore()
    for k in range(1, n):
        pl.semaphore_signal(barrier, inc=1, device_id={"frame": peer(k)}, device_id_type=MESH)
    for j in range(1, nh):
        pl.semaphore_signal(
            barrier, inc=1, device_id={"head": lax.rem(my_head + j, nh)}, device_id_type=MESH
        )
    pl.semaphore_wait(barrier, n + nh - 2)

    def text_at(p):
        part, block = lax.rem(p, split), p // split
        return (
            pl.ds(pl.multiple_of(part * text_part, text_part), text_part),
            pl.ds(pl.multiple_of(block * width, width), width),
        )

    sends = []
    for k in range(1, n):
        p = peer(k)
        for src, dst, sems in ((q, ql, q_sems), (g, gl, g_sems)):
            sends.append(frame_copy(src.at[text_at(p)], dst.at[me], sems, p, me, p))
            sends[-1].start()
    ql[me] = q[text_at(me)]
    gl[me] = g[text_at(me)]

    acc_k = acc_v = jnp.zeros((rows, cols), F32)
    for c in range(CHUNKS):
        loads[2 * c].wait()
        loads[2 * c + 1].wait()
        at = pl.ds(c * chunk, chunk)
        acc_k += jnp.dot(vis[:, at], wk[at], preferred_element_type=F32)
        acc_v += jnp.dot(vis[:, at], wv[at], preferred_element_type=F32)
    for a in range(kv_local):
        at = slice(a * HEAD_DIM, (a + 1) * HEAD_DIM)
        kvs[a, 0] = acc_k[:, at]
        kvs[a, 1] = acc_v[:, at]
    for k in range(1, n):
        p = peer(k)
        sends.append(frame_copy(kvs.at[p // share], kvl.at[me], kv_sems, p, me, p))
        sends[-1].start()
    kvl[me] = kvs[me // share]

    for p in range(n):
        visf[p] = vis[:, p * dn : (p + 1) * dn].astype(F32)

    def send_visual(first, sems):
        at = pl.ds(first, half)
        for k in range(1, n):
            p = peer(k)
            sends.append(frame_copy(visf.at[p, at], visl.at[me, at], sems, p, me, p))
            sends[-1].start()

    send_visual(0, v0_sems)

    def wait_all(land, sems):
        for k in range(1, n):
            s = source(k)
            frame_copy(land.at[s], land.at[s], sems, s, s, s).wait_recv()

    wait_all(ql, q_sems)
    wait_all(gl, g_sems)
    wait_all(kvl, kv_sems)

    keys = kvl[:, 0].reshape(n * rows, HEAD_DIM)
    values = kvl[:, 1].reshape(n * rows, HEAD_DIM)
    values2 = halves(values)
    keys_t = halves(keys.T)
    key_part = value_part = None
    for h in range(heads):
        at = slice(h * HEAD_DIM, (h + 1) * HEAD_DIM)
        query = ql[:, :, at].reshape(n * text_part, HEAD_DIM)
        grad = gl[:, :, at].reshape(n * text_part, HEAD_DIM)
        query2, grad2 = halves(query), halves(grad)
        scores = lax.dot_general(
            keys, query, (((1,), (1,)), ((), ())),
            precision=lax.Precision.HIGHEST, preferred_element_type=F32,
        ) * factor
        probs = jnp.exp(scores - jnp.max(scores, axis=0, keepdims=True))
        probs = probs * (1.0 / jnp.sum(probs, axis=0, keepdims=True))
        dprob = product(values2, grad2, ((1,), (1,)))
        delta = jnp.sum(probs * dprob, axis=0, keepdims=True)
        dscore2 = halves(probs * (dprob - delta))
        key_term = product(dscore2, query2, ((1,), (0,)))
        value_term = product(halves(probs), grad2, ((1,), (0,)))
        key_part = key_term if h == 0 else key_part + key_term
        value_part = value_term if h == 0 else value_part + value_term
        query_term = product(keys_t, dscore2, ((1,), (0,))).T * factor
        qgs[:, :, at] = query_term.reshape(n, text_part, HEAD_DIM)
    parts[:, 0] = key_part.reshape(n, rows, HEAD_DIM)
    parts[:, 1] = value_part.reshape(n, rows, HEAD_DIM)
    for k in range(1, n):
        p = peer(k)
        sends.append(frame_copy(parts.at[p], partl.at[me], part_sems, p, me, p))
        sends[-1].start()
    partl[me] = parts[me]
    send_visual(half, v1_sems)

    wait_all(partl, part_sems)
    low = []
    for i in range(2):
        columns = []
        for a in range(kv_local):
            total = partl[a * share, i]
            for p in range(a * share + 1, (a + 1) * share):
                total = total + partl[p, i]
            columns.append(total * factor if i == 0 else total)
        for a in range(kv_local):
            kgs[i, :, a * HEAD_DIM : (a + 1) * HEAD_DIM] = columns[a].astype(BF16).astype(F32)
        low.append(kgs[i].astype(BF16))

    def visual_term(p):
        at = pl.ds(pl.multiple_of(p * dh, dh), dh)
        dims = (((1,), (1,)), ((), ()))
        return lax.dot_general(
            low[0], wk[at], dims, preferred_element_type=F32
        ) + lax.dot_general(low[1], wv[at], dims, preferred_element_type=F32)

    order = sorted(range(1, nh), key=lambda j: -min(j, nh - j))
    for j in order:
        p = lax.rem(my_head + j, nh)
        vgp[p] = visual_term(p)
        sends.append(
            pltpu.make_async_remote_copy(
                src_ref=vgp.at[p], dst_ref=vgl.at[my_head], send_sem=z_sems.at[0, p],
                recv_sem=z_sems.at[1, my_head], device_id={"head": p}, device_id_type=MESH,
            )
        )
        sends[-1].start()
    for k in range(1, n):
        p = peer(k)
        sends.append(frame_copy(kgs, agl.at[me], ag_sems, p, me, p))
        sends[-1].start()
    for k in range(1, n):
        p = peer(k)
        sends.append(frame_copy(qgs.at[p], qgl.at[me], qg_sems, p, me, p))
        sends[-1].start()
    qgl[me] = qgs[me]
    agl[me] = kgs[...]
    vgl[my_head] = visual_term(my_head)

    def columns_of(s):
        return pl.ds(pl.multiple_of(s * rows, rows), rows)

    vist[:, columns_of(me)] = visf[me].T.astype(BF16)
    for k in range(1, n):
        s = source(k)
        for first, sems in ((0, v0_sems), (half, v1_sems)):
            land = visl.at[s, pl.ds(first, half)]
            frame_copy(land, land, sems, s, s, s).wait_recv()
        vist[:, columns_of(s)] = visl[s].T.astype(BF16)

    wait_all(agl, ag_sems)
    for i, out in enumerate((kwg_out, vwg_out)):
        out[...] = jnp.dot(
            vist[...], agl[:, i].reshape(n * rows, cols).astype(BF16), preferred_element_type=F32
        )
    wait_all(qgl, qg_sems)
    for s in range(n):
        part, block = s % split, s // split
        qg_out[
            part * text_part : (part + 1) * text_part, block * width : (block + 1) * width
        ] = qgl[s]

    for j in range(1, nh):
        s = lax.rem(my_head + nh - j, nh)
        pltpu.make_async_remote_copy(
            src_ref=vgl.at[s], dst_ref=vgl.at[s], send_sem=z_sems.at[0, s],
            recv_sem=z_sems.at[1, s], device_id={"head": s}, device_id_type=MESH,
        ).wait_recv()
    total = vgl[0]
    for p in range(1, nh):
        total = total + vgl[p]
    vg_out[...] = total
    for copy in sends:
        copy.wait_send()


def solution(mesh):
    n, nh = mesh.shape["frame"], mesh.shape["head"]

    def body(visual, w_key, w_value, queries, out_grad):
        rows, depth = visual.shape
        cols = w_key.shape[1]
        text, query_cols = queries.shape
        local_heads = query_cols // HEAD_DIM
        split = max(1, n // local_heads)
        part, width = text // split, query_cols * split // n
        vmem = pl.BlockSpec(memory_space=pltpu.VMEM)
        hbm = pl.BlockSpec(memory_space=pl.ANY)
        dn, dh = depth // n, depth // nh
        pairs = pltpu.SemaphoreType.DMA((2, n))
        return pl.pallas_call(
            functools.partial(kernel, n, nh),
            out_shape=(
                jax.ShapeDtypeStruct((text, query_cols), F32),
                jax.ShapeDtypeStruct((dn, cols), F32),
                jax.ShapeDtypeStruct((dn, cols), F32),
                jax.ShapeDtypeStruct((rows, dh), F32),
            ),
            in_specs=[vmem, hbm, hbm, vmem, vmem],
            out_specs=(vmem, vmem, vmem, vmem),
            scratch_shapes=[
                pltpu.VMEM((depth, cols), BF16),
                pltpu.VMEM((depth, cols), BF16),
                pltpu.VMEM((n, rows, dn), F32),
                pltpu.VMEM((n, rows, dn), F32),
                pltpu.VMEM((dn, n * rows), BF16),
                pltpu.VMEM((n, part, width), F32),
                pltpu.VMEM((n, part, width), F32),
                pltpu.VMEM((cols // HEAD_DIM, 2, rows, HEAD_DIM), F32),
                pltpu.VMEM((n, 2, rows, HEAD_DIM), F32),
                pltpu.VMEM((n, 2, rows, HEAD_DIM), F32),
                pltpu.VMEM((n, 2, rows, HEAD_DIM), F32),
                pltpu.VMEM((2, rows, cols), F32),
                pltpu.VMEM((n, 2, rows, cols), F32),
                pltpu.VMEM((n, part, width), F32),
                pltpu.VMEM((n, part, width), F32),
                pltpu.VMEM((nh, rows, dh), F32),
                pltpu.VMEM((nh, rows, dh), F32),
                pltpu.SemaphoreType.DMA((2, CHUNKS)),
                pairs, pairs, pairs, pairs, pairs, pairs, pairs, pairs,
                pltpu.SemaphoreType.DMA((2, nh)),
            ],
            compiler_params=pltpu.CompilerParams(
                collective_id=0, has_side_effects=True, vmem_limit_bytes=67000000
            ),
        )(visual, w_key, w_value, queries, out_grad)

    return jax.shard_map(
        body,
        mesh=mesh,
        in_specs=(
            P("frame", None),
            P(None, "head"),
            P(None, "head"),
            P("frame", "head"),
            P("frame", "head"),
        ),
        out_specs=(P("frame", "head"), P("frame", "head"), P("frame", "head"), P("frame", "head")),
        check_vma=False,
    )
```

time: 385 us -> 160 us (0.42)
  waiting for transfers between devices: 276 us -> 0 us
  Pallas kernels: 0 us -> 149 us
  matrix products: 50.9 us -> 0 us
  blocking collectives: 26.9 us -> 0 us
  between operations: 14.2 us -> 0.65 us
  local copies, waits for them, and re-layouts: 14.3 us -> 7.25 us
    reduce_scatter x4 -> x0, waiting for transfers between devices: 239 us -> none  [the longest x1 81 us: body(): lax.psum_scatter(visual_part, 'head', scatter_dimension=1, tiled=True)]
    pallas_call x0 -> x1, Pallas kernels: none -> 149 us  [body(): pl.pallas_call(functools.partial(kernel, n, nh), out_shape=(jax.ShapeDtyp...]
    dot_general x11 -> x0, matrix products: 50.9 us -> none  [the longest x1 6.54 us: finish(): jnp.einsum('agsn,nad->sagd', dscore, key_blk, precision=lax.Precision.HIG...]
    all_gather x2 -> x0, waiting for transfers between devices: 34.9 us -> none  [the longest x1 22.1 us: body(): lax.all_gather(queries, 'frame', axis=0, tiled=True)]
    all_gather x3 -> x0, blocking collectives: 26.9 us -> none  [combined_all(): gathered = jax.tree.map(lambda a: lax.all_gather(a, axis), part)]
    all_gather x2 -> x0, local copies, waits for them, and re-layouts: 5.89 us -> none  [the longest x1 2.99 us: body(): lax.all_gather(queries, 'frame', axis=0, tiled=True)]
  transfers between devices with their start and end apart: 6 -> 0, of which waited for: 6 -> 0; matrix products, arithmetic and copies ran while one was open for 12% -> 0% of each run, Pallas kernels for 0% -> 0%
where the time goes in v1:
time: 160 us; the launch traced here: 157 us
  Pallas kernels  149 us (93%)
  local copies, waits for them, and re-layouts  7.25 us (5%)
    pallas_call x1, Pallas kernels, body(): pl.pallas_call(functools.partial(kernel, n, nh), out_shape=(jax.ShapeDtyp...  149 us
    unnamed x6, local copies, waits for them, and re-layouts  7.25 us

profile of v1, /device:TPU:22, one launch (start us, length us, event | category | flops | bytes accessed | tf_op | source)
XLA Modules:
  0.0 157.4 jit_solution(8952002313075670009)
XLA Ops:
  0.6 149.5 %shard_map.84 = (f32[32,2048]{1,0:T(8,128)}, f32[1024,256]{1,0:T(8,128)}, f32[1024,256]{1,0:T(8,128)}, f32[128,2048]{1,0:T(8,128)}) custom-call(bf16[128,8192]{1,0:T(8,128)(2,1)} %vis.1, bf16[8192,256]{1,0:T(8,128)(2,1)} %wk_any.1, bf16[8192,256]{1,0:T(8,128)(2,1)} %wv_any.1, f32[32,2048]{1,0:T(8,128)} %q.1, f32[32,2048]{1,0:T(8,128)} %g.1), custom_call_target="tpu_custom_call" | custom-call | tf_op jit(solution)/shard_map/pallas_call | solution.py:257
  150.1 0.0 copy-start
  150.1 1.8 %copy.13 = f32[32,2048]{1,0:T(8,128)} copy(f32[32,2048]{1,0:T(8,128)} %get-tuple-element.8) | data formatting | bytes 524288
  151.9 2.3 %copy.14 = f32[1024,256]{1,0:T(8,128)} copy(f32[1024,256]{1,0:T(8,128)} %get-tuple-element.9) | data formatting | bytes 2097152
  154.2 2.3 %copy.15 = f32[1024,256]{1,0:T(8,128)} copy(f32[1024,256]{1,0:T(8,128)} %get-tuple-element.10) | data formatting | bytes 2097152
  156.4 0.0 copy-done
  156.4 1.0 copy.16
Async XLA Ops:
  150.1 6.3 %copy-start = (f32[128,2048]{1,0:T(8,128)S(1)}, f32[128,2048]{1,0:T(8,128)}, u32[]{:S(2)}) copy-start(f32[128,2048]{1,0:T(8,128)} %get-tuple-element.11) | copy-start | bytes 3145732

commit v2 on v1

--- a/solution.py
+++ b/solution.py
@@ -10,6 +10,7 @@
 HEAD_DIM = 128
 MESH = pl.DeviceIdType.MESH
 CHUNKS = 8
+PIECES = 4
 F32, BF16 = jnp.float32, jnp.bfloat16
 
 
@@ -28,8 +29,8 @@
 
 def kernel(
     n, nh, vis, wk_any, wv_any, q, g, qg_out, kwg_out, vwg_out, vg_out,
-    wk, wv, visf, visl, vist, ql, gl, kvs, kvl, parts, partl, kgs, agl, qgs, qgl, vgp, vgl,
-    w_sem, q_sems, g_sems, kv_sems, v0_sems, v1_sems, part_sems, qg_sems, ag_sems, z_sems,
+    wk, wv, visf, visl, vist, ql, gl, kvs, kvl, parts, partl, kgs, agl, qgs, qgl, vgp, zr, zl,
+    w_sem, q_sems, g_sems, kv_sems, v_sems, part_sems, qg_sems, ag_sems, z_sems,
 ):
     me, my_head = lax.axis_index("frame"), lax.axis_index("head")
     rows, depth = vis.shape
@@ -41,7 +42,8 @@
     share = n // kv_local
     dn, dh = depth // n, depth // nh
     chunk = depth // CHUNKS
-    half = rows // 2
+    bounds = (0, rows // 8, rows // 4, rows)
+    piece = rows // PIECES
     factor = HEAD_DIM ** (-0.5)
 
     def frame_copy(src, dst, sems, slot_send, slot_recv, target):
@@ -87,6 +89,24 @@
             sends[-1].start()
     ql[me] = q[text_at(me)]
     gl[me] = g[text_at(me)]
+
+    for p in range(n):
+        visf[p] = vis[:, p * dn : (p + 1) * dn].astype(F32)
+
+    def stretch(i):
+        return pl.ds(bounds[i], bounds[i + 1] - bounds[i])
+
+    def send_visual(i):
+        for k in range(1, n):
+            p = peer(k)
+            sends.append(
+                frame_copy(
+                    visf.at[p, stretch(i)], visl.at[me, stretch(i)], v_sems.at[i], p, me, p
+                )
+            )
+            sends[-1].start()
+
+    send_visual(0)
 
     acc_k = acc_v = jnp.zeros((rows, cols), F32)
     for c in range(CHUNKS):
@@ -105,17 +125,7 @@
         sends[-1].start()
     kvl[me] = kvs[me // share]
 
-    for p in range(n):
-        visf[p] = vis[:, p * dn : (p + 1) * dn].astype(F32)
-
-    def send_visual(first, sems):
-        at = pl.ds(first, half)
-        for k in range(1, n):
-            p = peer(k)
-            sends.append(frame_copy(visf.at[p, at], visl.at[me, at], sems, p, me, p))
-            sends[-1].start()
-
-    send_visual(0, v0_sems)
+    send_visual(1)
 
     def wait_all(land, sems):
         for k in range(1, n):
@@ -158,7 +168,12 @@
         sends.append(frame_copy(parts.at[p], partl.at[me], part_sems, p, me, p))
         sends[-1].start()
     partl[me] = parts[me]
-    send_visual(half, v1_sems)
+    for k in range(1, n):
+        p = peer(k)
+        sends.append(frame_copy(qgs.at[p], qgl.at[me], qg_sems, p, me, p))
+        sends[-1].start()
+    qgl[me] = qgs[me]
+    send_visual(2)
 
     wait_all(partl, part_sems)
     low = []
@@ -173,46 +188,71 @@
             kgs[i, :, a * HEAD_DIM : (a + 1) * HEAD_DIM] = columns[a].astype(BF16).astype(F32)
         low.append(kgs[i].astype(BF16))
 
+    for k in range(1, n):
+        p = peer(k)
+        sends.append(frame_copy(kgs, agl.at[me], ag_sems, p, me, p))
+        sends[-1].start()
+    agl[me] = kgs[...]
+
     def visual_term(p):
-        at = pl.ds(pl.multiple_of(p * dh, dh), dh)
+        at = slice(p * dh, (p + 1) * dh)
         dims = (((1,), (1,)), ((), ()))
-        return lax.dot_general(
+        vgp[p] = lax.dot_general(
             low[0], wk[at], dims, preferred_element_type=F32
         ) + lax.dot_general(low[1], wv[at], dims, preferred_element_type=F32)
 
-    order = sorted(range(1, nh), key=lambda j: -min(j, nh - j))
-    for j in order:
-        p = lax.rem(my_head + j, nh)
-        vgp[p] = visual_term(p)
-        sends.append(
-            pltpu.make_async_remote_copy(
-                src_ref=vgp.at[p], dst_ref=vgl.at[my_head], send_sem=z_sems.at[0, p],
-                recv_sem=z_sems.at[1, my_head], device_id={"head": p}, device_id_type=MESH,
-            )
-        )
-        sends[-1].start()
-    for k in range(1, n):
-        p = peer(k)
-        sends.append(frame_copy(kgs, agl.at[me], ag_sems, p, me, p))
-        sends[-1].start()
-    for k in range(1, n):
-        p = peer(k)
-        sends.append(frame_copy(qgs.at[p], qgl.at[me], qg_sems, p, me, p))
-        sends[-1].start()
-    qgl[me] = qgs[me]
-    agl[me] = kgs[...]
-    vgl[my_head] = visual_term(my_head)
+    def hop(way, d, i):
+        at = pl.ds(i * piece, piece)
+        land = zr if way == 0 else zl
+        return pltpu.make_async_remote_copy(
+            src_ref=vgp.at[d, at], dst_ref=land.at[d, at], send_sem=z_sems.at[way, 0, d, i],
+            recv_sem=z_sems.at[way, 1, d, i], device_id_type=MESH,
+            device_id={"head": jnp.clip(my_head + 1 - 2 * way, 0, nh - 1)},
+        )
+
+    def sends_to(way, d):
+        return my_head < d if way == 0 else my_head > d
+
+    def takes_from(way):
+        return my_head > 0 if way == 0 else my_head < nh - 1
+
+    def relay(way, d, i):
+        at = pl.ds(i * piece, piece)
+        land = zr if way == 0 else zl
+
+        @pl.when(sends_to(way, d))
+        def _():
+            @pl.when(takes_from(way))
+            def _():
+                hop(way, d, i).wait_recv()
+                vgp[d, at] += land[d, at]
+
+            hop(way, d, i).start()
 
     def columns_of(s):
         return pl.ds(pl.multiple_of(s * rows, rows), rows)
 
+    def take_visual(k):
+        s = source(k)
+        for i in range(3):
+            land = visl.at[s, stretch(i)]
+            frame_copy(land, land, v_sems.at[i], s, s, s).wait_recv()
+        vist[:, columns_of(s)] = visl[s].T.astype(BF16)
+
     vist[:, columns_of(me)] = visf[me].T.astype(BF16)
-    for k in range(1, n):
-        s = source(k)
-        for first, sems in ((0, v0_sems), (half, v1_sems)):
-            land = visl.at[s, pl.ds(first, half)]
-            frame_copy(land, land, sems, s, s, s).wait_recv()
-        vist[:, columns_of(s)] = visl[s].T.astype(BF16)
+    far = range(nh - 1, 0, -1)
+    left = list(range(1, n))
+    done = set()
+    for step, d in enumerate(far):
+        for way, at in ((0, d), (1, nh - 1 - d)):
+            if at not in done:
+                visual_term(at)
+                done.add(at)
+        for i in range(PIECES):
+            for way, at in ((0, d), (1, nh - 1 - d)):
+                relay(way, at, i)
+    for k in left:
+        take_visual(k)
 
     wait_all(agl, ag_sems)
     for i, out in enumerate((kwg_out, vwg_out)):
@@ -226,16 +266,22 @@
             part * text_part : (part + 1) * text_part, block * width : (block + 1) * width
         ] = qgl[s]
 
-    for j in range(1, nh):
-        s = lax.rem(my_head + nh - j, nh)
-        pltpu.make_async_remote_copy(
-            src_ref=vgl.at[s], dst_ref=vgl.at[s], send_sem=z_sems.at[0, s],
-            recv_sem=z_sems.at[1, s], device_id={"head": s}, device_id_type=MESH,
-        ).wait_recv()
-    total = vgl[0]
-    for p in range(1, nh):
-        total = total + vgl[p]
-    vg_out[...] = total
+    vg_out[...] = vgp[my_head]
+    for way, land in ((0, zr), (1, zl)):
+
+        @pl.when(takes_from(way))
+        def _():
+            for i in range(PIECES):
+                hop(way, my_head, i).wait_recv()
+            vg_out[...] += land[my_head]
+
+        for d in range(nh):
+
+            @pl.when(sends_to(way, d))
+            def _():
+                for i in range(PIECES):
+                    hop(way, d, i).wait_send()
+
     for copy in sends:
         copy.wait_send()
 
@@ -282,9 +328,12 @@
                 pltpu.VMEM((n, part, width), F32),
                 pltpu.VMEM((nh, rows, dh), F32),
                 pltpu.VMEM((nh, rows, dh), F32),
+                pltpu.VMEM((nh, rows, dh), F32),
                 pltpu.SemaphoreType.DMA((2, CHUNKS)),
-                pairs, pairs, pairs, pairs, pairs, pairs, pairs, pairs,
-                pltpu.SemaphoreType.DMA((2, nh)),
+                pairs, pairs, pairs,
+                pltpu.SemaphoreType.DMA((3, 2, n)),
+                pairs, pairs, pairs,
+                pltpu.SemaphoreType.DMA((2, 2, nh, PIECES)),
             ],
             compiler_params=pltpu.CompilerParams(
                 collective_id=0, has_side_effects=True, vmem_limit_bytes=67000000

time: 160 us -> 148 us (0.925); the launches traced: 157 us -> 147 us
  Pallas kernels: 149 us -> 139 us
    pallas_call x1, Pallas kernels: 149 us -> 139 us  [body(): pl.pallas_call(functools.partial(kernel, n, nh), out_shape=(jax.ShapeDtyp...]
where the time goes in v2:
time: 148 us; the launch traced here: 147 us
  Pallas kernels  139 us (94%)
  local copies, waits for them, and re-layouts  7.25 us (5%)
    pallas_call x1, Pallas kernels, body(): pl.pallas_call(functools.partial(kernel, n, nh), out_shape=(jax.ShapeDtyp...  139 us
    unnamed x6, local copies, waits for them, and re-layouts  7.25 us

profile of v2, /device:TPU:22, one launch (start us, length us, event | category | flops | bytes accessed | tf_op | source)
XLA Modules:
  0.0 147.3 jit_solution(9839864228219905772)
XLA Ops:
  0.6 139.4 %shard_map.84 = (f32[32,2048]{1,0:T(8,128)}, f32[1024,256]{1,0:T(8,128)}, f32[1024,256]{1,0:T(8,128)}, f32[128,2048]{1,0:T(8,128)}) custom-call(bf16[128,8192]{1,0:T(8,128)(2,1)} %vis.1, bf16[8192,256]{1,0:T(8,128)(2,1)} %wk_any.1, bf16[8192,256]{1,0:T(8,128)(2,1)} %wv_any.1, f32[32,2048]{1,0:T(8,128)} %q.1, f32[32,2048]{1,0:T(8,128)} %g.1), custom_call_target="tpu_custom_call" | custom-call | tf_op jit(solution)/shard_map/pallas_call | solution.py:303
  140.0 0.0 copy-start
  140.0 1.8 %copy.13 = f32[32,2048]{1,0:T(8,128)} copy(f32[32,2048]{1,0:T(8,128)} %get-tuple-element.8) | data formatting | bytes 524288
  141.8 2.3 %copy.14 = f32[1024,256]{1,0:T(8,128)} copy(f32[1024,256]{1,0:T(8,128)} %get-tuple-element.9) | data formatting | bytes 2097152
  144.0 2.3 %copy.15 = f32[1024,256]{1,0:T(8,128)} copy(f32[1024,256]{1,0:T(8,128)} %get-tuple-element.10) | data formatting | bytes 2097152
  146.3 0.0 copy-done
  146.3 1.0 copy.16
Async XLA Ops:
  140.0 6.3 %copy-start = (f32[128,2048]{1,0:T(8,128)S(1)}, f32[128,2048]{1,0:T(8,128)}, u32[]{:S(2)}) copy-start(f32[128,2048]{1,0:T(8,128)} %get-tuple-element.11) | copy-start | bytes 3145732

commit v3 on v2

--- a/solution.py
+++ b/solution.py
@@ -29,8 +29,8 @@
 
 def kernel(
     n, nh, vis, wk_any, wv_any, q, g, qg_out, kwg_out, vwg_out, vg_out,
-    wk, wv, visf, visl, vist, ql, gl, kvs, kvl, parts, partl, kgs, agl, qgs, qgl, vgp, zr, zl,
-    w_sem, q_sems, g_sems, kv_sems, v_sems, part_sems, qg_sems, ag_sems, z_sems,
+    wk, wv, visf, visl, vist, ql, gl, kvs, kvl, parts, pre, partl, kgs, agl, qgs, qgl, vgp, zr, zl,
+    w_sem, q_sems, g_sems, kv_sems, v_sems, pre_sem, part_sems, qg_sems, ag_sems, on_sems, z_sems,
 ):
     me, my_head = lax.axis_index("frame"), lax.axis_index("head")
     rows, depth = vis.shape
@@ -52,11 +52,50 @@
             recv_sem=sems.at[1, slot_recv], device_id={"frame": target}, device_id_type=MESH,
         )
 
+    def frame_copy_of(src, dst, send_sem, recv_sem, target):
+        return pltpu.make_async_remote_copy(
+            src_ref=src, dst_ref=dst, send_sem=send_sem, recv_sem=recv_sem,
+            device_id={"frame": target}, device_id_type=MESH,
+        )
+
     def peer(k):
         return lax.rem(me + k, n)
 
     def source(k):
         return lax.rem(me + n - k, n)
+
+    core, chip, chips = lax.rem(me, 2), me // 2, n // 2
+    sibling = me + 1 - 2 * core
+
+    def mate(j):
+        return lax.rem(me + 2 * j, n)
+
+    def mate_source(j):
+        return lax.rem(me + n - 2 * j, n)
+
+    def onward(land, sems, on, s):
+        return frame_copy_of(land.at[s], land.at[s], on.at[s], sems.at[1, s], sibling)
+
+    def spread(pick, land, sems):
+        sends.append(frame_copy(pick(sibling), land.at[me], sems, sibling, me, sibling))
+        sends[-1].start()
+        for j in range(1, chips):
+            p = mate(j)
+            sends.append(frame_copy(pick(p), land.at[me], sems, p, me, p))
+            sends[-1].start()
+
+    def forward(land, sems, on):
+        for j in range(1, chips):
+            s = mate_source(j)
+            frame_copy(land.at[s], land.at[s], sems, s, s, s).wait_recv()
+            sends.append(onward(land, sems, on, s))
+            sends[-1].start()
+
+    def wait_rest(land, sems):
+        frame_copy(land.at[sibling], land.at[sibling], sems, sibling, sibling, sibling).wait_recv()
+        for j in range(1, chips):
+            s = lax.rem(sibling + n - 2 * j, n)
+            frame_copy(land.at[s], land.at[s], sems, s, s, sibling).wait_recv()
 
     loads = []
     for c in range(CHUNKS):
@@ -119,10 +158,7 @@
         at = slice(a * HEAD_DIM, (a + 1) * HEAD_DIM)
         kvs[a, 0] = acc_k[:, at]
         kvs[a, 1] = acc_v[:, at]
-    for k in range(1, n):
-        p = peer(k)
-        sends.append(frame_copy(kvs.at[p // share], kvl.at[me], kv_sems, p, me, p))
-        sends[-1].start()
+    spread(lambda p: kvs.at[p // share], kvl, kv_sems)
     kvl[me] = kvs[me // share]
 
     send_visual(1)
@@ -132,9 +168,10 @@
             s = source(k)
             frame_copy(land.at[s], land.at[s], sems, s, s, s).wait_recv()
 
+    forward(kvl, kv_sems, on_sems.at[0])
     wait_all(ql, q_sems)
     wait_all(gl, g_sems)
-    wait_all(kvl, kv_sems)
+    wait_rest(kvl, kv_sems)
 
     keys = kvl[:, 0].reshape(n * rows, HEAD_DIM)
     values = kvl[:, 1].reshape(n * rows, HEAD_DIM)
@@ -161,13 +198,24 @@
         value_part = value_term if h == 0 else value_part + value_term
         query_term = product(keys_t, dscore2, ((1,), (0,))).T * factor
         qgs[:, :, at] = query_term.reshape(n, text_part, HEAD_DIM)
-    parts[:, 0] = key_part.reshape(n, rows, HEAD_DIM)
-    parts[:, 1] = value_part.reshape(n, rows, HEAD_DIM)
-    for k in range(1, n):
-        p = peer(k)
-        sends.append(frame_copy(parts.at[p], partl.at[me], part_sems, p, me, p))
+    for i, part in enumerate((key_part, value_part)):
+        part = part.reshape(chips, 2, rows, HEAD_DIM)
+        for c in range(2):
+            parts[c, :, i] = part[:, c]
+    exchange = frame_copy_of(
+        parts.at[1 - core], pre, pre_sem.at[0], pre_sem.at[1], sibling
+    )
+    exchange.start()
+    exchange.wait_recv()
+    sends.append(exchange)
+    parts[core] += pre[...]
+    for j in range(1, chips):
+        p = mate(j)
+        sends.append(
+            frame_copy(parts.at[core, p // 2], partl.at[chip], part_sems, p // 2, chip, p)
+        )
         sends[-1].start()
-    partl[me] = parts[me]
+    partl[chip] = parts[core, chip]
     for k in range(1, n):
         p = peer(k)
         sends.append(frame_copy(qgs.at[p], qgl.at[me], qg_sems, p, me, p))
@@ -175,23 +223,23 @@
     qgl[me] = qgs[me]
     send_visual(2)
 
-    wait_all(partl, part_sems)
+    for j in range(1, chips):
+        s = mate_source(j)
+        land = partl.at[s // 2]
+        frame_copy(land, land, part_sems, s // 2, s // 2, s).wait_recv()
     low = []
     for i in range(2):
         columns = []
         for a in range(kv_local):
-            total = partl[a * share, i]
-            for p in range(a * share + 1, (a + 1) * share):
+            total = partl[a * share // 2, i]
+            for p in range(a * share // 2 + 1, (a + 1) * share // 2):
                 total = total + partl[p, i]
             columns.append(total * factor if i == 0 else total)
         for a in range(kv_local):
             kgs[i, :, a * HEAD_DIM : (a + 1) * HEAD_DIM] = columns[a].astype(BF16).astype(F32)
         low.append(kgs[i].astype(BF16))
 
-    for k in range(1, n):
-        p = peer(k)
-        sends.append(frame_copy(kgs, agl.at[me], ag_sems, p, me, p))
-        sends[-1].start()
+    spread(lambda p: kgs, agl, ag_sems)
     agl[me] = kgs[...]
 
     def visual_term(p):
@@ -254,7 +302,8 @@
     for k in left:
         take_visual(k)
 
-    wait_all(agl, ag_sems)
+    forward(agl, ag_sems, on_sems.at[1])
+    wait_rest(agl, ag_sems)
     for i, out in enumerate((kwg_out, vwg_out)):
         out[...] = jnp.dot(
             vist[...], agl[:, i].reshape(n * rows, cols).astype(BF16), preferred_element_type=F32
@@ -320,8 +369,9 @@
                 pltpu.VMEM((n, part, width), F32),
                 pltpu.VMEM((cols // HEAD_DIM, 2, rows, HEAD_DIM), F32),
                 pltpu.VMEM((n, 2, rows, HEAD_DIM), F32),
-                pltpu.VMEM((n, 2, rows, HEAD_DIM), F32),
-                pltpu.VMEM((n, 2, rows, HEAD_DIM), F32),
+                pltpu.VMEM((2, n // 2, 2, rows, HEAD_DIM), F32),
+                pltpu.VMEM((n // 2, 2, rows, HEAD_DIM), F32),
+                pltpu.VMEM((n // 2, 2, rows, HEAD_DIM), F32),
                 pltpu.VMEM((2, rows, cols), F32),
                 pltpu.VMEM((n, 2, rows, cols), F32),
                 pltpu.VMEM((n, part, width), F32),
@@ -332,6 +382,8 @@
                 pltpu.SemaphoreType.DMA((2, CHUNKS)),
                 pairs, pairs, pairs,
                 pltpu.SemaphoreType.DMA((3, 2, n)),
+                pltpu.SemaphoreType.DMA((2,)),
+                pltpu.SemaphoreType.DMA((2, n // 2)),
                 pairs, pairs, pairs,
                 pltpu.SemaphoreType.DMA((2, 2, nh, PIECES)),
             ],

time: 148 us -> 138 us (0.932)
  Pallas kernels: 139 us -> 130 us
    pallas_call x1, Pallas kernels: 139 us -> 130 us  [body(): pl.pallas_call(functools.partial(kernel, n, nh), out_shape=(jax.ShapeDtyp...]
where the time goes in v3:
time: 138 us
  Pallas kernels  130 us (94%)
  local copies, waits for them, and re-layouts  7.25 us (5%)
    pallas_call x1, Pallas kernels, body(): pl.pallas_call(functools.partial(kernel, n, nh), out_shape=(jax.ShapeDtyp...  130 us
    unnamed x6, local copies, waits for them, and re-layouts  7.25 us

profile of v3, /device:TPU:22, one launch (start us, length us, event | category | flops | bytes accessed | tf_op | source)
XLA Modules:
  0.0 137.9 jit_solution(816874689070120354)
XLA Ops:
  0.6 130.0 %shard_map.84 = (f32[32,2048]{1,0:T(8,128)}, f32[1024,256]{1,0:T(8,128)}, f32[1024,256]{1,0:T(8,128)}, f32[128,2048]{1,0:T(8,128)}) custom-call(bf16[128,8192]{1,0:T(8,128)(2,1)} %vis.1, bf16[8192,256]{1,0:T(8,128)(2,1)} %wk_any.1, bf16[8192,256]{1,0:T(8,128)(2,1)} %wv_any.1, f32[32,2048]{1,0:T(8,128)} %q.1, f32[32,2048]{1,0:T(8,128)} %g.1), custom_call_target="tpu_custom_call" | custom-call | tf_op jit(solution)/shard_map/pallas_call | solution.py:352
  130.7 0.0 copy-start
  130.7 1.8 %copy.13 = f32[32,2048]{1,0:T(8,128)} copy(f32[32,2048]{1,0:T(8,128)} %get-tuple-element.8) | data formatting | bytes 524288
  132.4 2.3 %copy.14 = f32[1024,256]{1,0:T(8,128)} copy(f32[1024,256]{1,0:T(8,128)} %get-tuple-element.9) | data formatting | bytes 2097152
  134.7 2.3 %copy.15 = f32[1024,256]{1,0:T(8,128)} copy(f32[1024,256]{1,0:T(8,128)} %get-tuple-element.10) | data formatting | bytes 2097152
  137.0 0.0 copy-done
  137.0 1.0 copy.16
Async XLA Ops:
  130.7 6.3 %copy-start = (f32[128,2048]{1,0:T(8,128)S(1)}, f32[128,2048]{1,0:T(8,128)}, u32[]{:S(2)}) copy-start(f32[128,2048]{1,0:T(8,128)} %get-tuple-element.11) | copy-start | bytes 3145732

commit v4 on v3

--- a/solution.py
+++ b/solution.py
@@ -42,7 +42,7 @@
     share = n // kv_local
     dn, dh = depth // n, depth // nh
     chunk = depth // CHUNKS
-    bounds = (0, rows // 8, rows // 4, rows)
+    bounds = (0, rows)
     piece = rows // PIECES
     factor = HEAD_DIM ** (-0.5)
 
@@ -128,9 +128,6 @@
             sends[-1].start()
     ql[me] = q[text_at(me)]
     gl[me] = g[text_at(me)]
-
-    for p in range(n):
-        visf[p] = vis[:, p * dn : (p + 1) * dn].astype(F32)
 
     def stretch(i):
         return pl.ds(bounds[i], bounds[i + 1] - bounds[i])
@@ -144,8 +141,6 @@
                 )
             )
             sends[-1].start()
-
-    send_visual(0)
 
     acc_k = acc_v = jnp.zeros((rows, cols), F32)
     for c in range(CHUNKS):
@@ -161,13 +156,14 @@
     spread(lambda p: kvs.at[p // share], kvl, kv_sems)
     kvl[me] = kvs[me // share]
 
-    send_visual(1)
 
     def wait_all(land, sems):
         for k in range(1, n):
             s = source(k)
             frame_copy(land.at[s], land.at[s], sems, s, s, s).wait_recv()
 
+    for p in range(n):
+        visf[p] = vis[:, p * dn : (p + 1) * dn].astype(F32)
     forward(kvl, kv_sems, on_sems.at[0])
     wait_all(ql, q_sems)
     wait_all(gl, g_sems)
@@ -221,7 +217,7 @@
         sends.append(frame_copy(qgs.at[p], qgl.at[me], qg_sems, p, me, p))
         sends[-1].start()
     qgl[me] = qgs[me]
-    send_visual(2)
+    send_visual(0)
 
     for j in range(1, chips):
         s = mate_source(j)
@@ -282,7 +278,7 @@
 
     def take_visual(k):
         s = source(k)
-        for i in range(3):
+        for i in range(1):
             land = visl.at[s, stretch(i)]
             frame_copy(land, land, v_sems.at[i], s, s, s).wait_recv()
         vist[:, columns_of(s)] = visl[s].T.astype(BF16)
@@ -381,7 +377,7 @@
                 pltpu.VMEM((nh, rows, dh), F32),
                 pltpu.SemaphoreType.DMA((2, CHUNKS)),
                 pairs, pairs, pairs,
-                pltpu.SemaphoreType.DMA((3, 2, n)),
+                pltpu.SemaphoreType.DMA((1, 2, n)),
                 pltpu.SemaphoreType.DMA((2,)),
                 pltpu.SemaphoreType.DMA((2, n // 2)),
                 pairs, pairs, pairs,

time: 138 us -> 132 us (0.957)
  Pallas kernels: 130 us -> 124 us
    pallas_call x1, Pallas kernels: 130 us -> 124 us  [body(): pl.pallas_call(functools.partial(kernel, n, nh), out_shape=(jax.ShapeDtyp...]
where the time goes in v4:
time: 132 us
  Pallas kernels  124 us (94%)
  local copies, waits for them, and re-layouts  7.25 us (5%)
    pallas_call x1, Pallas kernels, body(): pl.pallas_call(functools.partial(kernel, n, nh), out_shape=(jax.ShapeDtyp...  124 us
    unnamed x6, local copies, waits for them, and re-layouts  7.25 us

profile of v4, /device:TPU:22, one launch (start us, length us, event | category | flops | bytes accessed | tf_op | source)
XLA Modules:
  0.0 131.7 jit_solution(14043826482876667856)
XLA Ops:
  0.6 123.8 %shard_map.84 = (f32[32,2048]{1,0:T(8,128)}, f32[1024,256]{1,0:T(8,128)}, f32[1024,256]{1,0:T(8,128)}, f32[128,2048]{1,0:T(8,128)}) custom-call(bf16[128,8192]{1,0:T(8,128)(2,1)} %vis.1, bf16[8192,256]{1,0:T(8,128)(2,1)} %wk_any.1, bf16[8192,256]{1,0:T(8,128)(2,1)} %wv_any.1, f32[32,2048]{1,0:T(8,128)} %q.1, f32[32,2048]{1,0:T(8,128)} %g.1), custom_call_target="tpu_custom_call" | custom-call | tf_op jit(solution)/shard_map/pallas_call | solution.py:348
  124.4 0.0 copy-start
  124.4 1.8 %copy.13 = f32[32,2048]{1,0:T(8,128)} copy(f32[32,2048]{1,0:T(8,128)} %get-tuple-element.8) | data formatting | bytes 524288
  126.2 2.3 %copy.14 = f32[1024,256]{1,0:T(8,128)} copy(f32[1024,256]{1,0:T(8,128)} %get-tuple-element.9) | data formatting | bytes 2097152
  128.5 2.3 %copy.15 = f32[1024,256]{1,0:T(8,128)} copy(f32[1024,256]{1,0:T(8,128)} %get-tuple-element.10) | data formatting | bytes 2097152
  130.7 0.0 copy-done
  130.7 1.0 copy.16
Async XLA Ops:
  124.4 6.3 %copy-start = (f32[128,2048]{1,0:T(8,128)S(1)}, f32[128,2048]{1,0:T(8,128)}, u32[]{:S(2)}) copy-start(f32[128,2048]{1,0:T(8,128)} %get-tuple-element.11) | copy-start | bytes 3145732
